TPU v7x, 32 devices: a whole 2x2x4 slice. The times are simulated.
32 devices in a mesh: tm: 8 (over y, x, core), rows: 4 (over z).
Axes of the slice: x: 2, y: 2, z: 4, core: 2. Of those that a mesh axis runs over, the one named last changes fastest.
Arguments:
- snapshots: bfloat16 [16384, 8192], P('tm', 'rows'), may hold values from -6 to 6
- spod_modes: bfloat16 [64, 2, 4, 8192], P('tm', None, None, 'rows'), may hold values from -0.09375 to 0.09375
- freq_index: int32 [64], replicated, may hold values from 1 to 128, as said below
- seg_offsets: int32 [4096], P('tm'), may hold values from 0 to 2047, as said below
Outputs:
- coefficients: float32 [64, 2, 4, 4096], P('rows', None, None, 'tm')
Inputs may be any that keep to these rules, and one draw needn't show every extreme that they name: Frequency f is bin freq_index[f] of a segment of 256 snapshots; values may repeat. Segment n starts at snapshot (n // 512) * 2048 + seg_offsets[n]; snapshots past the last one count as zeros.
All inputs are finite; a program needn't handle non-finite values.
Results may differ from a plain program's by a relative error of at most 0.0003.
Values may be sent and summed in bfloat16 or wider, within the bound.
No kernel may reach another device: no remote copies, remote signals or barrier semaphores. Data moves between devices by JAX's collectives and lax.ppermute only.
A program may use at most 64 MiB of HBM per device.

v0:
```python
import functools
import math

import jax
import jax.numpy as jnp
from jax import lax
from jax.experimental import pallas as pl
from jax.experimental.pallas import tpu as pltpu
from jax.sharding import PartitionSpec as P


M = 4
L = 256
ROWS = 2 * M
TOP = 32000.0
SPAN = 512
LANES = 128
MAGIC = 12582912.0


def swap(block, axis, distance):
    return lax.ppermute(block, axis, [(i, i ^ distance) for i in range(lax.axis_size(axis))])


def split(value):
    high = value.astype(jnp.bfloat16)
    return high, (value - high.astype(jnp.float32)).astype(jnp.bfloat16)


def dot(a, b, contract=((1,), (0,))):
    return lax.dot_general(a, b, (contract, ((), ())), preferred_element_type=jnp.float32)


def product3(data_high, data_low, weights_high, weights_low):
    return dot(data_high, weights_high) + dot(data_low, weights_high) + dot(data_high, weights_low)


def signs(width):
    real = lax.broadcasted_iota(jnp.int32, (ROWS, width), 0) < M
    return jnp.where(real, 1.0, -1.0).astype(jnp.float32)


VMEM = pl.BlockSpec(memory_space=pltpu.VMEM)
PARAMS = pltpu.CompilerParams(vmem_limit_bytes=20 * 2**20)


def kept(shape, kind):
    return pltpu.VMEM(shape, kind)


def hold(*values):
    return [pltpu.with_memory_space_constraint(value, pltpu.VMEM) for value in values]


def half_sine(phase_bin):
    centred = ((phase_bin + L // 2) & (L - 1)) - L // 2
    u = centred.astype(jnp.float32) * (math.pi / L)
    square = u * u
    sine = jnp.full_like(u, -1.0 / math.factorial(11))
    for k in (9, 7, 5, 3, 1):
        sine = sine * square + (-1.0) ** (k // 2) / math.factorial(k)
    return u, square, u * sine


def cos_sin(phase_bin):
    u, square, sine = half_sine(phase_bin)
    cosine = jnp.full_like(u, 1.0 / math.factorial(12))
    for k in (10, 8, 6, 4, 2, 0):
        cosine = cosine * square + (-1.0) ** (k // 2) / math.factorial(k)
    return 1.0 - 2.0 * sine * sine, 2.0 * sine * cosine


def prep_kernel(frequency_ref, snaps_ref, offsets_ref, *refs):
    out_ref, high_ref, low_ref, cos_ref, sin_ref, seg_cos_ref, seg_sin_ref = refs[:7]
    distance_ref, base_high, base_low, arrived = refs[7:]
    load = pltpu.make_async_copy(snaps_ref, out_ref, arrived)
    load.start()
    shape = base_high.shape
    distance = lax.broadcasted_iota(jnp.int32, shape, 0) - offsets_ref[...]
    _, _, sine = half_sine(distance)
    base_high[...], base_low[...] = split(math.sqrt(8.0 / (3.0 * L)) * (sine * sine))
    distance_ref[...] = distance.astype(jnp.int16)

    tm_pos = lax.axis_index("tm")
    groups, count = seg_cos_ref.shape
    n_tm = lax.axis_size("tm")
    each = groups // n_tm
    row = lax.broadcasted_iota(jnp.int32, (groups, LANES), 0)
    frequency = jnp.zeros((groups, LANES), jnp.int32)
    for i, d in enumerate(arrival(n_tm)):
        for f in range(each):
            frequency = jnp.where(row == i * each + f, frequency_ref[(d ^ tm_pos) * each + f], frequency)
    for at in range(0, L, LANES):
        cols = slice(at, at + LANES)
        moment = lax.broadcasted_iota(jnp.int32, (groups, LANES), 1) + at
        cos_ref[:, cols], sin_ref[:, cols] = cos_sin(frequency * moment)
    for at in range(0, count, LANES):
        cols = slice(at, at + LANES)
        seg_cos_ref[:, cols], seg_sin_ref[:, cols] = cos_sin(frequency * offsets_ref[:, cols])

    def block(step, _):
        distance = distance_ref[...] + (step * L).astype(jnp.int16)
        inside = (distance >= 0) & (distance < L)
        none = jnp.zeros(base_high.shape, jnp.bfloat16)
        rows = pl.ds(pl.multiple_of(step * L, L), L)
        high_ref[rows, :] = jnp.where(inside, base_high[...], none)
        low_ref[rows, :] = jnp.where(inside, base_low[...], none)
        return 0

    lax.fori_loop(0, high_ref.shape[0] // L, block, 0)
    load.wait()


def prep(snapshots, offsets, frequency, blocks):
    count, groups = offsets.shape[0], frequency.shape[0]
    weights = kept((blocks * L, count), jnp.bfloat16)
    theta = kept((groups, L), jnp.float32)
    phi = kept((groups, count), jnp.float32)
    return pl.pallas_call(
        prep_kernel,
        out_shape=(kept(snapshots.shape, snapshots.dtype), weights, weights, theta, theta, phi, phi),
        in_specs=[pl.BlockSpec(memory_space=pltpu.SMEM), pl.BlockSpec(memory_space=pltpu.HBM), VMEM],
        out_specs=(VMEM,) * 7,
        scratch_shapes=[pltpu.VMEM((L, count), kind) for kind in (jnp.int16, jnp.bfloat16, jnp.bfloat16)]
        + [pltpu.SemaphoreType.DMA],
        compiler_params=PARAMS,
        name="prep",
    )(frequency, pltpu.with_memory_space_constraint(snapshots, pltpu.HBM), offsets[None, :])


def span_kernel(pieces, groups, start, stop, span, *refs):
    refs = list(refs)
    piece_refs, refs = refs[:pieces], refs[pieces:]
    snaps_ref, cos_ref, sin_ref, wh_ref, wl_ref = refs[:5]
    refs = refs[5:]
    before_ref = refs.pop(0) if start else None
    acc_ref = refs.pop(0)
    head_ref = None if start else refs.pop(0)
    modes_ref, high_ref, low_ref = refs

    at = 0
    for ref in piece_refs:
        modes_ref[at : at + ref.shape[0], :] = ref[...]
        at += ref.shape[0]
    if start:
        acc_ref[...] = before_ref[...]
    sign = signs(L)

    def step(index, first):
        here = pl.ds(pl.multiple_of(index * span, span), span)
        projected = dot(modes_ref[...], snaps_ref[here, :], ((1,), (1,)))
        for g in range(acc_ref.shape[0] // ROWS // 2):
            rows = slice(2 * g * ROWS, (2 * g + 2) * ROWS)
            factors = []
            for f in (2 * g, 2 * g + 1):
                at = groups + f
                factors.append((sign * cos_ref[at : at + 1, :], -sin_ref[at : at + 1, :]))
            for b in range(span // L):
                cols = slice(b * L, (b + 1) * L)
                parts = []
                for u, (cosine, sine) in enumerate(factors):
                    f = 2 * g + u
                    x = projected[f * ROWS : (f + 1) * ROWS, cols]
                    parts.append(cosine * x + sine * pltpu.roll(x, M, 0))
                both = jnp.concatenate(parts, 0)
                if first and b == 0:
                    head_ref[rows, :] = both
                high_ref[rows, cols], low_ref[rows, cols] = split(both)
        part = product3(high_ref[...], low_ref[...], wh_ref[here, :], wl_ref[here, :])
        if first:
            acc_ref[...] = part
        else:
            acc_ref[...] += part

    if not start:
        step(0, True)
    if max(start, 1) < stop:
        lax.fori_loop(max(start, 1), stop, lambda index, _: (step(index, False), 0)[1], 0)


def spans(groups, pieces, snapshots, angles, high, low, start, stop, span, before=None):
    depth = snapshots.shape[1]
    rows = sum(piece.shape[0] for piece in pieces)
    count = high.shape[1]
    acc, head = kept((rows, count), jnp.float32), kept((rows, L), jnp.float32)
    inputs = [*pieces, snapshots, *angles[:2], high, low] + ([before] if start else [])
    return pl.pallas_call(
        functools.partial(span_kernel, len(pieces), groups, start, stop, span),
        out_shape=acc if start else (acc, head),
        in_specs=[VMEM] * len(inputs),
        out_specs=VMEM if start else (VMEM, VMEM),
        scratch_shapes=[pltpu.VMEM((rows, depth), jnp.bfloat16)] + [pltpu.VMEM((rows, span), jnp.bfloat16)] * 2,
        compiler_params=PARAMS,
        name="other_spans" if start else "first_spans",
    )(*hold(*inputs))


def code_kernel(per_dest, parts, *refs):
    refs = list(refs)
    acc_refs, halo_refs, refs = refs[:parts], refs[parts : 2 * parts], refs[2 * parts :]
    wh_ref, wl_ref, cos_ref, sin_ref, own_ref, *code_refs, full_ref, turned_ref = refs
    tm_pos, row_pos = lax.axis_index("tm"), lax.axis_index("rows")
    chunk, count = own_ref.shape
    block = chunk // per_dest
    n_tm = lax.axis_size("tm")
    shift = (tm_pos ^ (tm_pos + 1)) & (n_tm - 1)
    order = arrival(n_tm)
    spot = [order.index(d) for d in range(n_tm)]

    def row_of(distance):
        at = jnp.int32(0)
        for d in range(n_tm):
            at = jnp.where(distance == d, spot[d] * block, at)
        return pl.multiple_of(at, ROWS)

    at = 0
    for ref in halo_refs:
        turned_ref[at : at + ref.shape[0], :] = ref[...]
        at += ref.shape[0]
    at = 0
    last = pl.ds(wh_ref.shape[0] - L, L)
    for ref in acc_refs:
        rows = ref.shape[0]
        pieces = [turned_ref[pl.ds(row_of(order[at // block + i] ^ shift), block), :] for i in range(rows // block)]
        high, low = split(jnp.concatenate(pieces, 0))
        full_ref[at : at + rows, :] = ref[...] + product3(high, low, wh_ref[last, :], wl_ref[last, :])
        at += rows
    sign = signs(count)
    for f in range(cos_ref.shape[0]):
        rows = slice(f * ROWS, (f + 1) * ROWS)
        x = full_ref[rows, :]
        full_ref[rows, :] = cos_ref[f : f + 1, :] * x - (sign * sin_ref[f : f + 1, :]) * pltpu.roll(x, M, 0)
    lane = lax.broadcasted_iota(jnp.int32, (2 * ROWS, LANES), 1)
    for k in range(len(code_refs) + 1):
        for u in range(per_dest):
            at = row_of(((row_pos ^ k) * per_dest + u) ^ tm_pos)
            for r in range(0, block, 2 * ROWS):
                values = full_ref[pl.ds(pl.multiple_of(at + r, ROWS), 2 * ROWS), :]
                rows = slice(u * block + r, u * block + r + 2 * ROWS)
                if k == 0:
                    own_ref[rows, :] = values
                    continue
                peak = jnp.max(jnp.abs(values), axis=1, keepdims=True)
                power = jnp.ceil(jnp.log2(jnp.maximum(peak * (1.0 / TOP), 2.0**-126)))
                power = jnp.maximum(power, -126.0)
                codes = ((values * jnp.exp2(-power) + MAGIC) - MAGIC).astype(jnp.int32)
                bits = lax.shift_right_logical(jnp.broadcast_to(power.astype(jnp.int32) + 127, lane.shape), lane & 7) & 1
                front = codes[:, :LANES]
                front = jnp.where(lane < 8, (front & -2) | bits, front)
                code_refs[k - 1][rows, :LANES] = front.astype(jnp.int16)
                code_refs[k - 1][rows, LANES:] = codes[:, LANES:].astype(jnp.int16)


def rotate_and_code(accs, halos, high, low, angles, chunk, sends, per_dest):
    rows, count = sum(acc.shape[0] for acc in accs), accs[0].shape[1]
    code = kept((chunk, count), jnp.int16)
    return pl.pallas_call(
        functools.partial(code_kernel, per_dest, len(accs)),
        out_shape=(kept((chunk, count), jnp.float32),) + (code,) * sends,
        in_specs=[VMEM] * (2 * len(accs) + 4),
        out_specs=(VMEM,) * (sends + 1),
        scratch_shapes=[pltpu.VMEM((rows, count), jnp.float32), pltpu.VMEM((rows, L), jnp.float32)],
        compiler_params=PARAMS,
        name="rotate_and_code",
    )(*hold(*accs, *halos, high, low, *angles[2:]))


def sum_kernel(own_ref, *refs):
    *code_refs, out_ref = refs
    chunk, _ = own_ref.shape
    step = 2 * ROWS
    lane = lax.broadcasted_iota(jnp.int32, (step, LANES), 1)
    for r in range(0, chunk, step):
        rows = slice(r, r + step)
        total = own_ref[rows, :]
        for ref in code_refs:
            codes = ref[rows, :].astype(jnp.int32)
            bits = jnp.where(lane < 8, (codes[:, :LANES] & 1) << (lane & 7), 0)
            power = jnp.sum(bits.astype(jnp.float32), axis=1, keepdims=True) - 127.0
            total = total + codes.astype(jnp.float32) * jnp.exp2(power)
        for f in range(step // ROWS):
            for p in range(2):
                at = f * ROWS + p * M
                out_ref[r // ROWS + f, p] = total[at : at + M, :]


def add_up(own, codes):
    chunk, count = own.shape
    return pl.pallas_call(
        sum_kernel,
        out_shape=jax.ShapeDtypeStruct((chunk // ROWS, 2, M, count), jnp.float32),
        in_specs=[VMEM] * (1 + len(codes)),
        out_specs=VMEM,
        compiler_params=PARAMS,
        name="add_up",
    )(*hold(own, *codes))


def arrival(n_tm):
    return sorted(range(n_tm), key=lambda d: (d.bit_count(), d))


def after(values, earlier):
    return list(lax.optimization_barrier((*values, earlier)))[:-1]


def body(snapshots, spod_modes, freq_index, seg_offsets):
    time_len = snapshots.shape[0]
    n_tm = lax.axis_size("tm")
    n_rows = lax.axis_size("rows")
    per_device = spod_modes.shape[0]
    per_dest = n_tm // n_rows
    chunk = per_dest * per_device * ROWS
    span = math.gcd(SPAN, time_len)
    steps = time_len // span

    mine = spod_modes.reshape(per_device * ROWS, spod_modes.shape[3])
    blocks = {0: mine}
    chips = sorted(range(2, n_tm, 2), key=lambda d: d.bit_count())
    for d in chips:
        if d.bit_count() > 1:
            mine, *near = lax.optimization_barrier((mine, *(blocks[e] for e in chips if e.bit_count() < d.bit_count())))
            blocks.update(zip([e for e in chips if e.bit_count() < d.bit_count()], near))
        blocks[d] = swap(mine, "tm", d)
    for d in range(0, n_tm, 2):
        blocks[d + 1] = swap(blocks[d], "tm", 1)

    snapshots, high, low, *angles = prep(snapshots, seg_offsets, freq_index, time_len // L + 1)

    order = arrival(n_tm)
    route = [(i + 1, i) for i in range(n_tm - 1)]
    half = n_tm // 2
    pieces = [[blocks[d] for d in order[:half]], [blocks[d] for d in order[half:]]]
    first_acc, first_head = spans(0, pieces[0], snapshots, angles, high, low, 0, steps, span)
    pieces[1] = after(pieces[1], first_head)
    first_halo = lax.ppermute(first_head, "tm", route)
    at = half * per_device
    acc, head = spans(at, pieces[1], snapshots, angles, high, low, 0, 1, span)
    halo = lax.ppermute(head, "tm", route)
    acc = spans(at, pieces[1], snapshots, angles, high, low, 1, steps, span, before=acc)
    own, *codes = rotate_and_code([first_acc, acc], [first_halo, halo], high, low, angles, chunk, n_rows - 1, per_dest)
    return add_up(own, [swap(code, "rows", k + 1) for k, code in enumerate(codes)])


def solution(mesh):
    placed = (P("tm", "rows"), P("tm", None, None, "rows"), P(), P("tm"))
    return jax.shard_map(body, mesh=mesh, in_specs=placed, out_specs=P("rows", None, None, "tm"), check_vma=False)
```

profile of v0, /device:TPU:20, one launch (start us, length us, event | category | flops | bytes accessed | tf_op | source)
XLA Modules:
  0.0 57.0 jit_solution(9591479058516575845)
XLA Ops:
  0.0 1.0 %reshape.3.refs_0_ = bf16[64,2048]{1,0:T(8,128)(2,1)S(1)} reshape(bf16[8,2,4,2048]{3,2,1,0:T(4,128)(2,1)} %param.5) | data formatting | bytes 524288 | tf_op jit(solution)/shard_map/reshape | solution.py:317
  1.0 0.6 %collective-permute-start.2 = (bf16[64,2048]{1,0:T(8,128)(2,1)S(1)}, bf16[64,2048]{1,0:T(8,128)(2,1)S(1)}, u32[]{:S(2)}, u32[]{:S(2)}) collective-permute-start(bf16[64,2048]{1,0:T(8,128)(2,1)S(1)} %reshape.3.refs_0_), channel_id=1, source_target_pairs={{0,16},{4,20},{8,24},{12,28},{16,0},{20,4},{24,8},{28,12},{1,17},{... | collective-permute-start | bytes 786440 | tf_op jit(solution)/shard_map/ppermute | solution.py:22
  1.6 1.5 %collective-permute-start.1 = (bf16[64,2048]{1,0:T(8,128)(2,1)S(1)}, bf16[64,2048]{1,0:T(8,128)(2,1)S(1)}, u32[]{:S(2)}, u32[]{:S(2)}) collective-permute-start(bf16[64,2048]{1,0:T(8,128)(2,1)S(1)} %reshape.3.refs_0_), channel_id=1, source_target_pairs={{0,8},{4,12},{8,0},{12,4},{16,24},{20,28},{24,16},{28,20},{1,9},{5... | collective-permute-start | bytes 786440 | tf_op jit(solution)/shard_map/ppermute | solution.py:22
  3.1 6.0 %collective-permute-done.2.refs_3_ = bf16[64,2048]{1,0:T(8,128)(2,1)S(1)} collective-permute-done((bf16[64,2048]{1,0:T(8,128)(2,1)S(1)}, bf16[64,2048]{1,0:T(8,128)(2,1)S(1)}, u32[]{:S(2)}, u32[]{:S(2)}) %collective-permute-start.2) | collective-permute-done | bytes 262176 | tf_op jit(solution)/shard_map/ppermute | solution.py:22
  9.1 0.2 collective-permute-done.1.refs_2_
  9.4 2.4 %collective-permute-start.5 = (bf16[64,2048]{1,0:T(8,128)(2,1)S(1)}, bf16[64,2048]{1,0:T(8,128)(2,1)S(1)}, u32[]{:S(2)}, u32[]{:S(2)}) collective-permute-start(bf16[64,2048]{1,0:T(8,128)(2,1)S(1)} %reshape.3.refs_0_), channel_id=1, source_target_pairs={{0,24},{4,28},{8,16},{12,20},{16,8},{20,12},{24,0},{28,4},{1,25},{... | collective-permute-start | bytes 786440 | tf_op jit(solution)/shard_map/ppermute | solution.py:22
  11.8 0.0 collective-permute-start
  11.8 0.5 collective-permute-start.3
  12.3 0.0 collective-permute-start.4
  12.3 4.9 %collective-permute-done.5.refs_2_ = bf16[64,2048]{1,0:T(8,128)(2,1)S(1)} collective-permute-done((bf16[64,2048]{1,0:T(8,128)(2,1)S(1)}, bf16[64,2048]{1,0:T(8,128)(2,1)S(1)}, u32[]{:S(2)}, u32[]{:S(2)}) %collective-permute-start.5) | collective-permute-done | bytes 262176 | tf_op jit(solution)/shard_map/ppermute | solution.py:22
  17.2 0.0 collective-permute-start.6
  17.2 0.0 copy-start
  17.2 0.7 %copy-done = s32[512]{0:T(512)S(1)} copy-done((s32[512]{0:T(512)S(1)}, s32[512]{0:T(512)}, u32[]{:S(2)}) %copy-start) | copy-done | bytes 2072
  17.9 0.0 copy-start.1
  17.9 0.7 %copy-done.1 = s32[64]{0:T(128)S(1)} copy-done((s32[64]{0:T(128)S(1)}, s32[64]{0:T(128)}, u32[]{:S(2)}) %copy-start.1) | copy-done | bytes 280
  18.6 3.9 %prep.1 = (bf16[2048,2048]{1,0:T(8,128)(2,1)S(1)}, bf16[2304,512]{1,0:T(8,128)(2,1)S(1)}, bf16[2304,512]{1,0:T(8,128)(2,1)S(1)}, f32[64,256]{1,0:T(8,128)S(1)}, ...) custom-call(s32[64]{0:T(128)S(1)} %copy-done.1, bf16[2048,2048]{1,0:T(8,128)(2,1)} %snaps_ref.1, ...), custom_call_target="tpu_custom_call" | custom-call | tf_op jit(solution)/shard_map/prep/pallas_call | solution.py:119
  22.5 0.0 collective-permute-done.refs_1_
  22.5 5.2 %first_spans.2 = (f32[256,512]{1,0:T(8,128)S(1)}, f32[256,256]{1,0:T(8,128)S(1)}) custom-call(bf16[64,2048]{1,0:T(8,128)(2,1)S(1)} %reshape.3.refs_0_, bf16[64,2048]{1,0:T(8,128)(2,1)S(1)} %collective-permute-done.refs_1_, bf16[64,2048]{1,0:T(8,128)(2,1)S(1)} %collective-permute-done.1.refs_2_, bf16[64,2048]{1,0:T(8,128)(2,1)S(1)} %collective-permute-done.2.refs_3_, ...), custom_call_target="tpu_custom_call" | custom-call | tf_op jit(solution)/shard_map/first_spans/pallas_call | solution.py:187
  27.8 4.4 %collective-permute-start.7 = (f32[256,256]{1,0:T(8,128)S(1)}, f32[256,256]{1,0:T(8,128)S(1)}, u32[]{:S(2)}, u32[]{:S(2)}) collective-permute-start(f32[256,256]{1,0:T(8,128)S(1)} %get-tuple-element.36), channel_id=1, source_target_pairs={{4,0},{8,4},{12,8},{16,12},{20,16},{24,20},{28,24},{5,1},{9,5},{13... | collective-permute-start | bytes 786440 | tf_op jit(solution)/shard_map/ppermute | solution.py:336
  32.2 0.0 collective-permute-done.3.refs_0_
  32.2 0.0 collective-permute-done.4.refs_1_
  32.2 0.0 collective-permute-done.6.refs_3_
  32.2 1.3 %first_spans.3 = (f32[256,512]{1,0:T(8,128)S(1)}, f32[256,256]{1,0:T(8,128)S(1)}) custom-call(bf16[64,2048]{1,0:T(8,128)(2,1)S(1)} %collective-permute-done.3.refs_0_, bf16[64,2048]{1,0:T(8,128)(2,1)S(1)} %collective-permute-done.4.refs_1_, bf16[64,2048]{1,0:T(8,128)(2,1)S(1)} %collective-permute-done.5.refs_2_, ...), custom_call_target="tpu_custom_call" | custom-call | tf_op jit(solution)/shard_map/first_spans/pallas_call | solution.py:187
  33.5 1.9 %collective-permute-start.8 = (f32[256,256]{1,0:T(8,128)S(1)}, f32[256,256]{1,0:T(8,128)S(1)}, u32[]{:S(2)}, u32[]{:S(2)}) collective-permute-start(f32[256,256]{1,0:T(8,128)S(1)} %get-tuple-element.42), channel_id=1, source_target_pairs={{4,0},{8,4},{12,8},{16,12},{20,16},{24,20},{28,24},{5,1},{9,5},{13... | collective-permute-start | bytes 786440 | tf_op jit(solution)/shard_map/ppermute | solution.py:339
  35.4 3.9 %other_spans.1.refs_1_ = f32[256,512]{1,0:T(8,128)S(1)} custom-call(bf16[64,2048]{1,0:T(8,128)(2,1)S(1)} %collective-permute-done.3.refs_0_, bf16[64,2048]{1,0:T(8,128)(2,1)S(1)} %collective-permute-done.4.refs_1_, bf16[64,2048]{1,0:T(8,128)(2,1)S(1)} %collective-permute-done.5.refs_2_, bf16[64,2048]{1,0:T(8,128)(2,1)S(1)} %collective-permute-done.6.refs_3_, ...), custom_call_target="tpu_custom_call" | custom-call | tf_op jit(solution)/shard_map/other_spans/pallas_call | solution.py:187
  39.3 0.0 collective-permute-done.7.refs_2_
  39.3 0.0 collective-permute-done.8.refs_3_
  39.4 1.1 %rotate_and_code.1 = (f32[128,512]{1,0:T(8,128)S(1)}, s16[128,512]{1,0:T(8,128)(2,1)S(1)}, s16[128,512]{1,0:T(8,128)(2,1)S(1)}, s16[128,512]{1,0:T(8,128)(2,1)S(1)}) custom-call(f32[256,512]{1,0:T(8,128)S(1)} %get-tuple-element.34.refs_0_, f32[256,512]{1,0:T(8,128)S(1)} %other_spans.1.refs_1_, f32[256,256]{1,0:T(8,128)S(1)} %collective-permute-done.7.refs_2_, ...), custom_call_target="tpu_custom_call" | custom-call | tf_op jit(solution)/shard_map/rotate_and_code/pallas_call | solution.py:257
  40.5 1.6 %collective-permute-start.9 = (s16[128,512]{1,0:T(8,128)(2,1)S(1)}, s16[128,512]{1,0:T(8,128)(2,1)S(1)}, u32[]{:S(2)}, u32[]{:S(2)}) collective-permute-start(s16[128,512]{1,0:T(8,128)(2,1)S(1)} %get-tuple-element.46), channel_id=1, source_target_pairs={{0,1},{1,0},{2,3},{3,2},{4,5},{5,4},{6,7},{7,6},{8,9},{9,8},{10,11... | collective-permute-start | bytes 393224 | tf_op jit(solution)/shard_map/ppermute | solution.py:22
  42.1 0.4 collective-permute-start.10
  42.4 1.6 %collective-permute-start.11 = (s16[128,512]{1,0:T(8,128)(2,1)S(1)}, s16[128,512]{1,0:T(8,128)(2,1)S(1)}, u32[]{:S(2)}, u32[]{:S(2)}) collective-permute-start(s16[128,512]{1,0:T(8,128)(2,1)S(1)} %get-tuple-element.48), channel_id=1, source_target_pairs={{0,3},{1,2},{2,1},{3,0},{4,7},{5,6},{6,5},{7,4},{8,11},{9,10},{10,... | collective-permute-start | bytes 393224 | tf_op jit(solution)/shard_map/ppermute | solution.py:22
  44.0 3.1 %collective-permute-done.9.refs_0_ = s16[128,512]{1,0:T(8,128)(2,1)S(1)} collective-permute-done((s16[128,512]{1,0:T(8,128)(2,1)S(1)}, s16[128,512]{1,0:T(8,128)(2,1)S(1)}, u32[]{:S(2)}, u32[]{:S(2)}) %collective-permute-start.9) | collective-permute-done | bytes 131104 | tf_op jit(solution)/shard_map/ppermute | solution.py:22
  47.1 4.9 %collective-permute-done.10.refs_1_ = s16[128,512]{1,0:T(8,128)(2,1)S(1)} collective-permute-done((s16[128,512]{1,0:T(8,128)(2,1)S(1)}, s16[128,512]{1,0:T(8,128)(2,1)S(1)}, u32[]{:S(2)}, u32[]{:S(2)}) %collective-permute-start.10) | collective-permute-done | bytes 131104 | tf_op jit(solution)/shard_map/ppermute | solution.py:22
  52.0 4.1 %collective-permute-done.11.refs_2_ = s16[128,512]{1,0:T(8,128)(2,1)S(1)} collective-permute-done((s16[128,512]{1,0:T(8,128)(2,1)S(1)}, s16[128,512]{1,0:T(8,128)(2,1)S(1)}, u32[]{:S(2)}, u32[]{:S(2)}) %collective-permute-start.11) | collective-permute-done | bytes 131104 | tf_op jit(solution)/shard_map/ppermute | solution.py:22
  56.1 0.9 %add_up.1 = f32[16,2,4,512]{3,2,1,0:T(4,128)} custom-call(f32[128,512]{1,0:T(8,128)S(1)} %get-tuple-element.45.own_ref, s16[128,512]{1,0:T(8,128)(2,1)S(1)} %collective-permute-done.9.refs_0_, s16[128,512]{1,0:T(8,128)(2,1)S(1)} %collective-permute-done.10.refs_1_, s16[128,512]{1,0:T(8,128)(2,1)S(1)} %collective-permute-done.11.refs_2_), custom_call_target="tpu_custom_call" | custom-call | tf_op jit(solution)/shard_map/add_up/pallas_call | solution.py:289
Async XLA Ops:
  1.0 8.1 %collective-permute-start.2 = (bf16[64,2048]{1,0:T(8,128)(2,1)S(1)}, bf16[64,2048]{1,0:T(8,128)(2,1)S(1)}, u32[]{:S(2)}, u32[]{:S(2)}) collective-permute-start(bf16[64,2048]{1,0:T(8,128)(2,1)S(1)} %reshape.3.refs_0_), channel_id=1, source_target_pairs={{0,16},{4,20},{8,24},{12,28},{16,0},{20,4},{24,8},{28,12},{1,17},{... | collective-permute-start | bytes 786440 | tf_op jit(solution)/shard_map/ppermute | solution.py:22
  1.6 7.8 %collective-permute-start.1 = (bf16[64,2048]{1,0:T(8,128)(2,1)S(1)}, bf16[64,2048]{1,0:T(8,128)(2,1)S(1)}, u32[]{:S(2)}, u32[]{:S(2)}) collective-permute-start(bf16[64,2048]{1,0:T(8,128)(2,1)S(1)} %reshape.3.refs_0_), channel_id=1, source_target_pairs={{0,8},{4,12},{8,0},{12,4},{16,24},{20,28},{24,16},{28,20},{1,9},{5... | collective-permute-start | bytes 786440 | tf_op jit(solution)/shard_map/ppermute | solution.py:22
  9.4 7.9 %collective-permute-start.5 = (bf16[64,2048]{1,0:T(8,128)(2,1)S(1)}, bf16[64,2048]{1,0:T(8,128)(2,1)S(1)}, u32[]{:S(2)}, u32[]{:S(2)}) collective-permute-start(bf16[64,2048]{1,0:T(8,128)(2,1)S(1)} %reshape.3.refs_0_), channel_id=1, source_target_pairs={{0,24},{4,28},{8,16},{12,20},{16,8},{20,12},{24,0},{28,4},{1,25},{... | collective-permute-start | bytes 786440 | tf_op jit(solution)/shard_map/ppermute | solution.py:22
  11.8 10.7 %collective-permute-start = (bf16[64,2048]{1,0:T(8,128)(2,1)S(1)}, bf16[64,2048]{1,0:T(8,128)(2,1)S(1)}, u32[]{:S(2)}, u32[]{:S(2)}) collective-permute-start(bf16[64,2048]{1,0:T(8,128)(2,1)S(1)} %reshape.3.refs_0_), channel_id=1, source_target_pairs={{0,4},{4,0},{8,12},{12,8},{16,20},{20,16},{24,28},{28,24},{1,5},{5... | collective-permute-start | bytes 786440 | tf_op jit(solution)/shard_map/ppermute | solution.py:22
  11.8 20.4 %collective-permute-start.3 = (bf16[64,2048]{1,0:T(8,128)(2,1)S(1)}, bf16[64,2048]{1,0:T(8,128)(2,1)S(1)}, u32[]{:S(2)}, u32[]{:S(2)}) collective-permute-start(bf16[64,2048]{1,0:T(8,128)(2,1)S(1)} %collective-permute-done.1.refs_2_), channel_id=1, source_target_pairs={{0,4},{4,0},{8,12},{12,8},{16,20},{20,16},{24,28},{28,24},{1,5},{5... | collective-permute-start | bytes 786440 | tf_op jit(solution)/shard_map/ppermute | solution.py:22
  12.3 19.9 %collective-permute-start.4 = (bf16[64,2048]{1,0:T(8,128)(2,1)S(1)}, bf16[64,2048]{1,0:T(8,128)(2,1)S(1)}, u32[]{:S(2)}, u32[]{:S(2)}) collective-permute-start(bf16[64,2048]{1,0:T(8,128)(2,1)S(1)} %collective-permute-done.2.refs_3_), channel_id=1, source_target_pairs={{0,4},{4,0},{8,12},{12,8},{16,20},{20,16},{24,28},{28,24},{1,5},{5... | collective-permute-start | bytes 786440 | tf_op jit(solution)/shard_map/ppermute | solution.py:22
  17.2 15.0 %collective-permute-start.6 = (bf16[64,2048]{1,0:T(8,128)(2,1)S(1)}, bf16[64,2048]{1,0:T(8,128)(2,1)S(1)}, u32[]{:S(2)}, u32[]{:S(2)}) collective-permute-start(bf16[64,2048]{1,0:T(8,128)(2,1)S(1)} %collective-permute-done.5.refs_2_), channel_id=1, source_target_pairs={{0,4},{4,0},{8,12},{12,8},{16,20},{20,16},{24,28},{28,24},{1,5},{5... | collective-permute-start | bytes 786440 | tf_op jit(solution)/shard_map/ppermute | solution.py:22
  17.2 0.7 %copy-start = (s32[512]{0:T(512)S(1)}, s32[512]{0:T(512)}, u32[]{:S(2)}) copy-start(s32[512]{0:T(512)} %param.7) | copy-start | bytes 6148
  17.9 0.7 %copy-start.1 = (s32[64]{0:T(128)S(1)}, s32[64]{0:T(128)}, u32[]{:S(2)}) copy-start(s32[64]{0:T(128)} %frequency_ref.1) | copy-start | bytes 772
  27.8 11.6 %collective-permute-start.7 = (f32[256,256]{1,0:T(8,128)S(1)}, f32[256,256]{1,0:T(8,128)S(1)}, u32[]{:S(2)}, u32[]{:S(2)}) collective-permute-start(f32[256,256]{1,0:T(8,128)S(1)} %get-tuple-element.36), channel_id=1, source_target_pairs={{4,0},{8,4},{12,8},{16,12},{20,16},{24,20},{28,24},{5,1},{9,5},{13... | collective-permute-start | bytes 786440 | tf_op jit(solution)/shard_map/ppermute | solution.py:336
  33.5 5.9 %collective-permute-start.8 = (f32[256,256]{1,0:T(8,128)S(1)}, f32[256,256]{1,0:T(8,128)S(1)}, u32[]{:S(2)}, u32[]{:S(2)}) collective-permute-start(f32[256,256]{1,0:T(8,128)S(1)} %get-tuple-element.42), channel_id=1, source_target_pairs={{4,0},{8,4},{12,8},{16,12},{20,16},{24,20},{28,24},{5,1},{9,5},{13... | collective-permute-start | bytes 786440 | tf_op jit(solution)/shard_map/ppermute | solution.py:339
  40.5 6.6 %collective-permute-start.9 = (s16[128,512]{1,0:T(8,128)(2,1)S(1)}, s16[128,512]{1,0:T(8,128)(2,1)S(1)}, u32[]{:S(2)}, u32[]{:S(2)}) collective-permute-start(s16[128,512]{1,0:T(8,128)(2,1)S(1)} %get-tuple-element.46), channel_id=1, source_target_pairs={{0,1},{1,0},{2,3},{3,2},{4,5},{5,4},{6,7},{7,6},{8,9},{9,8},{10,11... | collective-permute-start | bytes 393224 | tf_op jit(solution)/shard_map/ppermute | solution.py:22
  42.1 9.9 %collective-permute-start.10 = (s16[128,512]{1,0:T(8,128)(2,1)S(1)}, s16[128,512]{1,0:T(8,128)(2,1)S(1)}, u32[]{:S(2)}, u32[]{:S(2)}) collective-permute-start(s16[128,512]{1,0:T(8,128)(2,1)S(1)} %get-tuple-element.47), channel_id=1, source_target_pairs={{0,2},{1,3},{2,0},{3,1},{4,6},{5,7},{6,4},{7,5},{8,10},{9,11},{10,... | collective-permute-start | bytes 393224 | tf_op jit(solution)/shard_map/ppermute | solution.py:22
  42.4 13.6 %collective-permute-start.11 = (s16[128,512]{1,0:T(8,128)(2,1)S(1)}, s16[128,512]{1,0:T(8,128)(2,1)S(1)}, u32[]{:S(2)}, u32[]{:S(2)}) collective-permute-start(s16[128,512]{1,0:T(8,128)(2,1)S(1)} %get-tuple-element.48), channel_id=1, source_target_pairs={{0,3},{1,2},{2,1},{3,0},{4,7},{5,6},{6,5},{7,4},{8,11},{9,10},{10,... | collective-permute-start | bytes 393224 | tf_op jit(solution)/shard_map/ppermute | solution.py:22
where the time goes:
time: 57.2 us; the launch traced here: 57 us
  waiting for transfers between devices  23.3 us (41%)
  Pallas kernels  16.3 us (28%)
  starting transfers between devices  14.9 us (26%)
  local copies, waits for them, and re-layouts  2.35 us (4%)
    ppermute x10, waiting for transfers between devices, swap(): lax.ppermute(block, axis, [(i, i ^ distance) for i in range(lax.axis_size...  23.3 us
    pallas_call x3, Pallas kernels, spans(): pl.pallas_call(functools.partial(span_kernel, len(pieces), groups, start,...  10.4 us
    ppermute x10, starting transfers between devices, swap(): lax.ppermute(block, axis, [(i, i ^ distance) for i in range(lax.axis_size...  8.58 us
    ppermute x1, starting transfers between devices, body(): first_halo = lax.ppermute(first_head, 'tm', route)  4.41 us
    pallas_call x1, Pallas kernels, prep(): pl.pallas_call(prep_kernel, out_shape=(kept(snapshots.shape, snapshots.dt...  3.93 us
    ppermute x1, starting transfers between devices, body(): halo = lax.ppermute(head, 'tm', route)  1.93 us
    unnamed x4, local copies, waits for them, and re-layouts  1.34 us
  transfers between devices with their start and end apart: 12, of which 6 were waited for; matrix products, arithmetic and copies ran while one was open for 0% of the time, Pallas kernels for 25%

commit v1 on v0

--- a/solution.py
+++ b/solution.py
@@ -13,7 +13,7 @@
 L = 256
 ROWS = 2 * M
 TOP = 32000.0
-SPAN = 512
+SPAN = 1024
 LANES = 128
 MAGIC = 12582912.0
 
@@ -128,77 +128,123 @@
     )(frequency, pltpu.with_memory_space_constraint(snapshots, pltpu.HBM), offsets[None, :])
 
 
-def span_kernel(pieces, groups, start, stop, span, *refs):
-    refs = list(refs)
-    piece_refs, refs = refs[:pieces], refs[pieces:]
-    snaps_ref, cos_ref, sin_ref, wh_ref, wl_ref = refs[:5]
-    refs = refs[5:]
-    before_ref = refs.pop(0) if start else None
-    acc_ref = refs.pop(0)
-    head_ref = None if start else refs.pop(0)
-    modes_ref, high_ref, low_ref = refs
-
+def gathered(piece_refs, modes_ref):
     at = 0
     for ref in piece_refs:
         modes_ref[at : at + ref.shape[0], :] = ref[...]
         at += ref.shape[0]
-    if start:
-        acc_ref[...] = before_ref[...]
+    return modes_ref[...]
+
+
+def demodulated(projected, cos_ref, sin_ref, groups, put):
     sign = signs(L)
-
-    def step(index, first):
-        here = pl.ds(pl.multiple_of(index * span, span), span)
-        projected = dot(modes_ref[...], snaps_ref[here, :], ((1,), (1,)))
-        for g in range(acc_ref.shape[0] // ROWS // 2):
-            rows = slice(2 * g * ROWS, (2 * g + 2) * ROWS)
-            factors = []
-            for f in (2 * g, 2 * g + 1):
-                at = groups + f
-                factors.append((sign * cos_ref[at : at + 1, :], -sin_ref[at : at + 1, :]))
-            for b in range(span // L):
-                cols = slice(b * L, (b + 1) * L)
-                parts = []
-                for u, (cosine, sine) in enumerate(factors):
-                    f = 2 * g + u
-                    x = projected[f * ROWS : (f + 1) * ROWS, cols]
-                    parts.append(cosine * x + sine * pltpu.roll(x, M, 0))
-                both = jnp.concatenate(parts, 0)
-                if first and b == 0:
-                    head_ref[rows, :] = both
-                high_ref[rows, cols], low_ref[rows, cols] = split(both)
+    for g in range(projected.shape[0] // ROWS // 2):
+        rows = slice(2 * g * ROWS, (2 * g + 2) * ROWS)
+        factors = []
+        for f in (2 * g, 2 * g + 1):
+            at = groups + f
+            factors.append((sign * cos_ref[at : at + 1, :], -sin_ref[at : at + 1, :]))
+        for b in range(projected.shape[1] // L):
+            cols = slice(b * L, (b + 1) * L)
+            parts = []
+            for u, (cosine, sine) in enumerate(factors):
+                f = 2 * g + u
+                x = projected[f * ROWS : (f + 1) * ROWS, cols]
+                parts.append(cosine * x + sine * pltpu.roll(x, M, 0))
+            put(rows, cols, jnp.concatenate(parts, 0))
+
+
+def span_kernel(pieces, groups, span, with_head, *refs):
+    piece_refs, refs = refs[:pieces], refs[pieces:]
+    snaps_ref, cos_ref, sin_ref, wh_ref, wl_ref, acc_ref = refs[:6]
+    head_ref = refs[6] if with_head else None
+    modes_ref, high_ref, low_ref = refs[-3:]
+    modes = gathered(piece_refs, modes_ref)
+
+    for index in range(snaps_ref.shape[0] // span):
+        here = slice(index * span, (index + 1) * span)
+
+        def put(rows, cols, both):
+            if with_head and index == 0 and cols.start == 0:
+                head_ref[rows, :] = both
+            high_ref[rows, cols], low_ref[rows, cols] = split(both)
+
+        demodulated(dot(modes, snaps_ref[here, :], ((1,), (1,))), cos_ref, sin_ref, groups, put)
         part = product3(high_ref[...], low_ref[...], wh_ref[here, :], wl_ref[here, :])
-        if first:
+        if index == 0:
             acc_ref[...] = part
         else:
             acc_ref[...] += part
 
-    if not start:
-        step(0, True)
-    if max(start, 1) < stop:
-        lax.fori_loop(max(start, 1), stop, lambda index, _: (step(index, False), 0)[1], 0)
-
-
-def spans(groups, pieces, snapshots, angles, high, low, start, stop, span, before=None):
+
+def spans(groups, pieces, snapshots, angles, high, low, span, with_head):
     depth = snapshots.shape[1]
     rows = sum(piece.shape[0] for piece in pieces)
-    count = high.shape[1]
-    acc, head = kept((rows, count), jnp.float32), kept((rows, L), jnp.float32)
-    inputs = [*pieces, snapshots, *angles[:2], high, low] + ([before] if start else [])
-    return pl.pallas_call(
-        functools.partial(span_kernel, len(pieces), groups, start, stop, span),
-        out_shape=acc if start else (acc, head),
+    acc, head = kept((rows, high.shape[1]), jnp.float32), kept((rows, L), jnp.float32)
+    inputs = [*pieces, snapshots, *angles[:2], high, low]
+    return pl.pallas_call(
+        functools.partial(span_kernel, len(pieces), groups, span, with_head),
+        out_shape=(acc, head) if with_head else acc,
         in_specs=[VMEM] * len(inputs),
-        out_specs=VMEM if start else (VMEM, VMEM),
+        out_specs=(VMEM, VMEM) if with_head else VMEM,
         scratch_shapes=[pltpu.VMEM((rows, depth), jnp.bfloat16)] + [pltpu.VMEM((rows, span), jnp.bfloat16)] * 2,
         compiler_params=PARAMS,
-        name="other_spans" if start else "first_spans",
+        name="spans",
+    )(*hold(*inputs))
+
+
+def encode(values):
+    peak = jnp.max(jnp.abs(values), axis=1, keepdims=True)
+    power = jnp.ceil(jnp.log2(jnp.maximum(peak * (1.0 / TOP), 2.0**-126)))
+    power = jnp.maximum(power, -126.0)
+    codes = ((values * jnp.exp2(-power) + MAGIC) - MAGIC).astype(jnp.int32)
+    lane = lax.broadcasted_iota(jnp.int32, (values.shape[0], LANES), 1)
+    bits = lax.shift_right_logical(jnp.broadcast_to(power.astype(jnp.int32) + 127, lane.shape), lane & 7) & 1
+    front = codes[:, :LANES]
+    front = jnp.where(lane < 8, (front & -2) | bits, front)
+    return front.astype(jnp.int16), codes[:, LANES:].astype(jnp.int16)
+
+
+def decode(codes):
+    codes = codes.astype(jnp.int32)
+    lane = lax.broadcasted_iota(jnp.int32, (codes.shape[0], LANES), 1)
+    bits = jnp.where(lane < 8, (codes[:, :LANES] & 1) << (lane & 7), 0)
+    power = jnp.sum(bits.astype(jnp.float32), axis=1, keepdims=True) - 127.0
+    return codes.astype(jnp.float32) * jnp.exp2(power)
+
+
+def head_kernel(pieces, groups, *refs):
+    piece_refs, (snaps_ref, cos_ref, sin_ref, before_ref, code_ref, modes_ref) = refs[:pieces], refs[pieces:]
+    start = before_ref.shape[0]
+    for r in range(0, start, 2 * ROWS):
+        rows = slice(r, r + 2 * ROWS)
+        code_ref[rows, :LANES], code_ref[rows, LANES:] = encode(before_ref[rows, :])
+
+    def put(rows, cols, both):
+        rows = slice(start + rows.start, start + rows.stop)
+        code_ref[rows, :LANES], code_ref[rows, LANES:] = encode(both)
+
+    demodulated(dot(gathered(piece_refs, modes_ref), snaps_ref[:L, :], ((1,), (1,))), cos_ref, sin_ref, groups, put)
+
+
+def heads(groups, pieces, snapshots, angles, before):
+    rows = sum(piece.shape[0] for piece in pieces)
+    inputs = [*pieces, snapshots, *angles[:2], before]
+    return pl.pallas_call(
+        functools.partial(head_kernel, len(pieces), groups),
+        out_shape=kept((before.shape[0] + rows, L), jnp.int16),
+        in_specs=[VMEM] * len(inputs),
+        out_specs=VMEM,
+        scratch_shapes=[pltpu.VMEM((rows, snapshots.shape[1]), jnp.bfloat16)],
+        compiler_params=PARAMS,
+        name="heads",
     )(*hold(*inputs))
 
 
 def code_kernel(per_dest, parts, *refs):
     refs = list(refs)
-    acc_refs, halo_refs, refs = refs[:parts], refs[parts : 2 * parts], refs[2 * parts :]
-    wh_ref, wl_ref, cos_ref, sin_ref, own_ref, *code_refs, full_ref, turned_ref = refs
+    acc_refs, refs = refs[:parts], refs[parts:]
+    halo_ref, wh_ref, wl_ref, cos_ref, sin_ref, own_ref, *code_refs, full_ref, turned_ref = refs
     tm_pos, row_pos = lax.axis_index("tm"), lax.axis_index("rows")
     chunk, count = own_ref.shape
     block = chunk // per_dest
@@ -211,26 +257,22 @@
         at = jnp.int32(0)
         for d in range(n_tm):
             at = jnp.where(distance == d, spot[d] * block, at)
-        return pl.multiple_of(at, ROWS)
-
+        return pl.multiple_of(at, 2 * ROWS)
+
+    for i, d in enumerate(order):
+        turned_ref[i * block : (i + 1) * block, :] = decode(halo_ref[pl.ds(row_of(d ^ shift), block), :])
+    last = slice(wh_ref.shape[0] - L, wh_ref.shape[0])
     at = 0
-    for ref in halo_refs:
-        turned_ref[at : at + ref.shape[0], :] = ref[...]
-        at += ref.shape[0]
-    at = 0
-    last = pl.ds(wh_ref.shape[0] - L, L)
     for ref in acc_refs:
-        rows = ref.shape[0]
-        pieces = [turned_ref[pl.ds(row_of(order[at // block + i] ^ shift), block), :] for i in range(rows // block)]
-        high, low = split(jnp.concatenate(pieces, 0))
-        full_ref[at : at + rows, :] = ref[...] + product3(high, low, wh_ref[last, :], wl_ref[last, :])
-        at += rows
+        rows = slice(at, at + ref.shape[0])
+        high, low = split(turned_ref[rows, :])
+        full_ref[rows, :] = ref[...] + product3(high, low, wh_ref[last, :], wl_ref[last, :])
+        at = rows.stop
     sign = signs(count)
     for f in range(cos_ref.shape[0]):
         rows = slice(f * ROWS, (f + 1) * ROWS)
         x = full_ref[rows, :]
         full_ref[rows, :] = cos_ref[f : f + 1, :] * x - (sign * sin_ref[f : f + 1, :]) * pltpu.roll(x, M, 0)
-    lane = lax.broadcasted_iota(jnp.int32, (2 * ROWS, LANES), 1)
     for k in range(len(code_refs) + 1):
         for u in range(per_dest):
             at = row_of(((row_pos ^ k) * per_dest + u) ^ tm_pos)
@@ -239,45 +281,33 @@
                 rows = slice(u * block + r, u * block + r + 2 * ROWS)
                 if k == 0:
                     own_ref[rows, :] = values
-                    continue
-                peak = jnp.max(jnp.abs(values), axis=1, keepdims=True)
-                power = jnp.ceil(jnp.log2(jnp.maximum(peak * (1.0 / TOP), 2.0**-126)))
-                power = jnp.maximum(power, -126.0)
-                codes = ((values * jnp.exp2(-power) + MAGIC) - MAGIC).astype(jnp.int32)
-                bits = lax.shift_right_logical(jnp.broadcast_to(power.astype(jnp.int32) + 127, lane.shape), lane & 7) & 1
-                front = codes[:, :LANES]
-                front = jnp.where(lane < 8, (front & -2) | bits, front)
-                code_refs[k - 1][rows, :LANES] = front.astype(jnp.int16)
-                code_refs[k - 1][rows, LANES:] = codes[:, LANES:].astype(jnp.int16)
-
-
-def rotate_and_code(accs, halos, high, low, angles, chunk, sends, per_dest):
+                else:
+                    code_refs[k - 1][rows, :LANES], code_refs[k - 1][rows, LANES:] = encode(values)
+
+
+def rotate_and_code(accs, halo, high, low, angles, chunk, sends, per_dest):
     rows, count = sum(acc.shape[0] for acc in accs), accs[0].shape[1]
     code = kept((chunk, count), jnp.int16)
     return pl.pallas_call(
         functools.partial(code_kernel, per_dest, len(accs)),
         out_shape=(kept((chunk, count), jnp.float32),) + (code,) * sends,
-        in_specs=[VMEM] * (2 * len(accs) + 4),
+        in_specs=[VMEM] * (len(accs) + 5),
         out_specs=(VMEM,) * (sends + 1),
         scratch_shapes=[pltpu.VMEM((rows, count), jnp.float32), pltpu.VMEM((rows, L), jnp.float32)],
         compiler_params=PARAMS,
         name="rotate_and_code",
-    )(*hold(*accs, *halos, high, low, *angles[2:]))
+    )(*hold(*accs, halo, high, low, *angles[2:]))
 
 
 def sum_kernel(own_ref, *refs):
     *code_refs, out_ref = refs
     chunk, _ = own_ref.shape
     step = 2 * ROWS
-    lane = lax.broadcasted_iota(jnp.int32, (step, LANES), 1)
     for r in range(0, chunk, step):
         rows = slice(r, r + step)
         total = own_ref[rows, :]
         for ref in code_refs:
-            codes = ref[rows, :].astype(jnp.int32)
-            bits = jnp.where(lane < 8, (codes[:, :LANES] & 1) << (lane & 7), 0)
-            power = jnp.sum(bits.astype(jnp.float32), axis=1, keepdims=True) - 127.0
-            total = total + codes.astype(jnp.float32) * jnp.exp2(power)
+            total = total + decode(ref[rows, :])
         for f in range(step // ROWS):
             for p in range(2):
                 at = f * ROWS + p * M
@@ -312,7 +342,6 @@
     per_dest = n_tm // n_rows
     chunk = per_dest * per_device * ROWS
     span = math.gcd(SPAN, time_len)
-    steps = time_len // span
 
     mine = spod_modes.reshape(per_device * ROWS, spod_modes.shape[3])
     blocks = {0: mine}
@@ -331,15 +360,17 @@
     route = [(i + 1, i) for i in range(n_tm - 1)]
     half = n_tm // 2
     pieces = [[blocks[d] for d in order[:half]], [blocks[d] for d in order[half:]]]
-    first_acc, first_head = spans(0, pieces[0], snapshots, angles, high, low, 0, steps, span)
+    first_acc, first_head = spans(0, pieces[0], snapshots, angles, high, low, span, True)
     pieces[1] = after(pieces[1], first_head)
-    first_halo = lax.ppermute(first_head, "tm", route)
     at = half * per_device
-    acc, head = spans(at, pieces[1], snapshots, angles, high, low, 0, 1, span)
-    halo = lax.ppermute(head, "tm", route)
-    acc = spans(at, pieces[1], snapshots, angles, high, low, 1, steps, span, before=acc)
-    own, *codes = rotate_and_code([first_acc, acc], [first_halo, halo], high, low, angles, chunk, n_rows - 1, per_dest)
-    return add_up(own, [swap(code, "rows", k + 1) for k, code in enumerate(codes)])
+    codes = heads(at, pieces[1], snapshots, angles, first_head)
+    halo = lax.ppermute(codes, "tm", route)
+    [snapshots] = after([snapshots], codes)
+    acc = spans(at, pieces[1], snapshots, angles, high, low, span, False)
+    own, *codes = rotate_and_code([first_acc, acc], halo, high, low, angles, chunk, n_rows - 1, per_dest)
+    for k, code in enumerate(codes):
+        codes[k] = swap(code, "rows", k + 1)
+    return add_up(own, codes)
 
 
 def solution(mesh):

time: 57.2 us -> 53.7 us (0.939)
  the two profiles are of different devices: /device:TPU:20 before, /device:TPU:11 now
where the time goes in v1:
time: 53.7 us; the launch traced here: 53.5 us
  waiting for transfers between devices  22.6 us (42%)
  Pallas kernels  14.9 us (28%)
  starting transfers between devices  13.6 us (25%)
  local copies, waits for them, and re-layouts  2.35 us (4%)
    ppermute x10, waiting for transfers between devices, swap(): lax.ppermute(block, axis, [(i, i ^ distance) for i in range(lax.axis_size...  20.1 us
    ppermute x10, starting transfers between devices, swap(): lax.ppermute(block, axis, [(i, i ^ distance) for i in range(lax.axis_size...  11.7 us
    pallas_call x2, Pallas kernels, spans(): pl.pallas_call(functools.partial(span_kernel, len(pieces), groups, span,...  8.25 us
    pallas_call x1, Pallas kernels, prep(): pl.pallas_call(prep_kernel, out_shape=(kept(snapshots.shape, snapshots.dt...  3.93 us
    ppermute x1, waiting for transfers between devices, body(): halo = lax.ppermute(codes, 'tm', route)  2.52 us
    ppermute x1, starting transfers between devices, body(): halo = lax.ppermute(codes, 'tm', route)  1.92 us
    unnamed x4, local copies, waits for them, and re-layouts  1.34 us
    pallas_call x1, Pallas kernels, rotate_and_code(): pl.pallas_call(functools.partial(code_kernel, per_dest, len(accs)), out_s...  1.15 us
  transfers between devices with their start and end apart: 11, of which 6 were waited for; matrix products, arithmetic and copies ran while one was open for 0% of the time, Pallas kernels for 23%

profile of v1, /device:TPU:11, one launch (start us, length us, event | category | flops | bytes accessed | tf_op | source)
XLA Modules:
  0.0 53.5 jit_solution(11532886136311953627)
XLA Ops:
  0.0 1.0 %reshape.3.refs_0_ = bf16[64,2048]{1,0:T(8,128)(2,1)S(1)} reshape(bf16[8,2,4,2048]{3,2,1,0:T(4,128)(2,1)} %param.5) | data formatting | bytes 524288 | tf_op jit(solution)/shard_map/reshape | solution.py:346
  1.0 0.3 collective-permute-start.1
  1.3 1.2 %collective-permute-start.2 = (bf16[64,2048]{1,0:T(8,128)(2,1)S(1)}, bf16[64,2048]{1,0:T(8,128)(2,1)S(1)}, u32[]{:S(2)}, u32[]{:S(2)}) collective-permute-start(bf16[64,2048]{1,0:T(8,128)(2,1)S(1)} %reshape.3.refs_0_), channel_id=1, source_target_pairs={{0,16},{4,20},{8,24},{12,28},{16,0},{20,4},{24,8},{28,12},{1,17},{... | collective-permute-start | bytes 786440 | tf_op jit(solution)/shard_map/ppermute | solution.py:22
  2.6 5.7 %collective-permute-done.1.refs_2_ = bf16[64,2048]{1,0:T(8,128)(2,1)S(1)} collective-permute-done((bf16[64,2048]{1,0:T(8,128)(2,1)S(1)}, bf16[64,2048]{1,0:T(8,128)(2,1)S(1)}, u32[]{:S(2)}, u32[]{:S(2)}) %collective-permute-start.1) | collective-permute-done | bytes 262176 | tf_op jit(solution)/shard_map/ppermute | solution.py:22
  8.3 0.0 collective-permute-done.2.refs_3_
  8.3 2.1 %collective-permute-start.5 = (bf16[64,2048]{1,0:T(8,128)(2,1)S(1)}, bf16[64,2048]{1,0:T(8,128)(2,1)S(1)}, u32[]{:S(2)}, u32[]{:S(2)}) collective-permute-start(bf16[64,2048]{1,0:T(8,128)(2,1)S(1)} %reshape.3.refs_0_), channel_id=1, source_target_pairs={{0,24},{4,28},{8,16},{12,20},{16,8},{20,12},{24,0},{28,4},{1,25},{... | collective-permute-start | bytes 786440 | tf_op jit(solution)/shard_map/ppermute | solution.py:22
  10.4 2.1 %collective-permute-start = (bf16[64,2048]{1,0:T(8,128)(2,1)S(1)}, bf16[64,2048]{1,0:T(8,128)(2,1)S(1)}, u32[]{:S(2)}, u32[]{:S(2)}) collective-permute-start(bf16[64,2048]{1,0:T(8,128)(2,1)S(1)} %reshape.3.refs_0_), channel_id=1, source_target_pairs={{0,4},{4,0},{8,12},{12,8},{16,20},{20,16},{24,28},{28,24},{1,5},{5... | collective-permute-start | bytes 786440 | tf_op jit(solution)/shard_map/ppermute | solution.py:22
  12.5 0.0 collective-permute-start.3
  12.5 0.5 collective-permute-start.4
  13.0 2.2 %collective-permute-done.5.refs_2_ = bf16[64,2048]{1,0:T(8,128)(2,1)S(1)} collective-permute-done((bf16[64,2048]{1,0:T(8,128)(2,1)S(1)}, bf16[64,2048]{1,0:T(8,128)(2,1)S(1)}, u32[]{:S(2)}, u32[]{:S(2)}) %collective-permute-start.5) | collective-permute-done | bytes 262176 | tf_op jit(solution)/shard_map/ppermute | solution.py:22
  15.3 2.6 %collective-permute-start.6 = (bf16[64,2048]{1,0:T(8,128)(2,1)S(1)}, bf16[64,2048]{1,0:T(8,128)(2,1)S(1)}, u32[]{:S(2)}, u32[]{:S(2)}) collective-permute-start(bf16[64,2048]{1,0:T(8,128)(2,1)S(1)} %collective-permute-done.5.refs_2_), channel_id=1, source_target_pairs={{0,4},{4,0},{8,12},{12,8},{16,20},{20,16},{24,28},{28,24},{1,5},{5... | collective-permute-start | bytes 786440 | tf_op jit(solution)/shard_map/ppermute | solution.py:22
  17.9 0.0 copy-start
  17.9 0.7 %copy-done = s32[512]{0:T(512)S(1)} copy-done((s32[512]{0:T(512)S(1)}, s32[512]{0:T(512)}, u32[]{:S(2)}) %copy-start) | copy-done | bytes 2072
  18.6 0.0 copy-start.1
  18.6 0.7 %copy-done.1 = s32[64]{0:T(128)S(1)} copy-done((s32[64]{0:T(128)S(1)}, s32[64]{0:T(128)}, u32[]{:S(2)}) %copy-start.1) | copy-done | bytes 280
  19.2 3.9 %prep.1 = (bf16[2048,2048]{1,0:T(8,128)(2,1)S(1)}, bf16[2304,512]{1,0:T(8,128)(2,1)S(1)}, bf16[2304,512]{1,0:T(8,128)(2,1)S(1)}, f32[64,256]{1,0:T(8,128)S(1)}, ...) custom-call(s32[64]{0:T(128)S(1)} %copy-done.1, bf16[2048,2048]{1,0:T(8,128)(2,1)} %snaps_ref.1, ...), custom_call_target="tpu_custom_call" | custom-call | tf_op jit(solution)/shard_map/prep/pallas_call | solution.py:119
  23.2 0.0 collective-permute-done.refs_1_
  23.2 4.1 %spans.2 = (f32[256,512]{1,0:T(8,128)S(1)}, f32[256,256]{1,0:T(8,128)S(1)}) custom-call(bf16[64,2048]{1,0:T(8,128)(2,1)S(1)} %reshape.3.refs_0_, bf16[64,2048]{1,0:T(8,128)(2,1)S(1)} %collective-permute-done.refs_1_, bf16[64,2048]{1,0:T(8,128)(2,1)S(1)} %collective-permute-done.1.refs_2_, bf16[64,2048]{1,0:T(8,128)(2,1)S(1)} %collective-permute-done.2.refs_3_, ...), custom_call_target="tpu_custom_call" | custom-call | tf_op jit(solution)/shard_map/spans/pallas_call | solution.py:185
  27.3 0.0 collective-permute-done.3.refs_0_
  27.3 0.0 collective-permute-done.4.refs_1_
  27.3 0.0 collective-permute-done.6.refs_3_
  27.3 0.7 %heads.1 = s16[512,256]{1,0:T(8,128)(2,1)S(1)} custom-call(bf16[64,2048]{1,0:T(8,128)(2,1)S(1)} %collective-permute-done.3.refs_0_, bf16[64,2048]{1,0:T(8,128)(2,1)S(1)} %collective-permute-done.4.refs_1_, bf16[64,2048]{1,0:T(8,128)(2,1)S(1)} %collective-permute-done.5.refs_2_, bf16[64,2048]{1,0:T(8,128)(2,1)S(1)} %collective-permute-done.6.refs_3_, ...), custom_call_target="tpu_custom_call" | custom-call | tf_op jit(solution)/shard_map/heads/pallas_call | solution.py:233
  28.0 1.9 %collective-permute-start.7 = (s16[512,256]{1,0:T(8,128)(2,1)S(1)}, s16[512,256]{1,0:T(8,128)(2,1)S(1)}, u32[]{:S(2)}, u32[]{:S(2)}) collective-permute-start(s16[512,256]{1,0:T(8,128)(2,1)S(1)} %heads.1), channel_id=1, source_target_pairs={{4,0},{8,4},{12,8},{16,12},{20,16},{24,20},{28,24},{5,1},{9,5},{13... | collective-permute-start | bytes 786440 | tf_op jit(solution)/shard_map/ppermute | solution.py:367
  30.0 4.1 %spans.3.refs_1_ = f32[256,512]{1,0:T(8,128)S(1)} custom-call(bf16[64,2048]{1,0:T(8,128)(2,1)S(1)} %collective-permute-done.3.refs_0_, bf16[64,2048]{1,0:T(8,128)(2,1)S(1)} %collective-permute-done.4.refs_1_, bf16[64,2048]{1,0:T(8,128)(2,1)S(1)} %collective-permute-done.5.refs_2_, bf16[64,2048]{1,0:T(8,128)(2,1)S(1)} %collective-permute-done.6.refs_3_, ...), custom_call_target="tpu_custom_call" | custom-call | tf_op jit(solution)/shard_map/spans/pallas_call | solution.py:185
  34.1 2.5 %collective-permute-done.7.refs_2_ = s16[512,256]{1,0:T(8,128)(2,1)S(1)} collective-permute-done((s16[512,256]{1,0:T(8,128)(2,1)S(1)}, s16[512,256]{1,0:T(8,128)(2,1)S(1)}, u32[]{:S(2)}, u32[]{:S(2)}) %collective-permute-start.7) | collective-permute-done | bytes 262176 | tf_op jit(solution)/shard_map/ppermute | solution.py:367
  36.6 1.2 %rotate_and_code.1 = (f32[128,512]{1,0:T(8,128)S(1)}, s16[128,512]{1,0:T(8,128)(2,1)S(1)}, s16[128,512]{1,0:T(8,128)(2,1)S(1)}, s16[128,512]{1,0:T(8,128)(2,1)S(1)}) custom-call(f32[256,512]{1,0:T(8,128)S(1)} %get-tuple-element.33.refs_0_, f32[256,512]{1,0:T(8,128)S(1)} %spans.3.refs_1_, s16[512,256]{1,0:T(8,128)(2,1)S(1)} %collective-permute-done.7.refs_2_, ...), custom_call_target="tpu_custom_call" | custom-call | tf_op jit(solution)/shard_map/rotate_and_code/pallas_call | solution.py:291
  37.8 0.3 collective-permute-start.8
  38.1 2.2 %collective-permute-start.9 = (s16[128,512]{1,0:T(8,128)(2,1)S(1)}, s16[128,512]{1,0:T(8,128)(2,1)S(1)}, u32[]{:S(2)}, u32[]{:S(2)}) collective-permute-start(s16[128,512]{1,0:T(8,128)(2,1)S(1)} %get-tuple-element.45), channel_id=1, source_target_pairs={{0,2},{1,3},{2,0},{3,1},{4,6},{5,7},{6,4},{7,5},{8,10},{9,11},{10,... | collective-permute-start | bytes 393224 | tf_op jit(solution)/shard_map/ppermute | solution.py:22
  40.3 0.2 collective-permute-start.10
  40.5 2.3 %collective-permute-done.8.refs_0_ = s16[128,512]{1,0:T(8,128)(2,1)S(1)} collective-permute-done((s16[128,512]{1,0:T(8,128)(2,1)S(1)}, s16[128,512]{1,0:T(8,128)(2,1)S(1)}, u32[]{:S(2)}, u32[]{:S(2)}) %collective-permute-start.8) | collective-permute-done | bytes 131104 | tf_op jit(solution)/shard_map/ppermute | solution.py:22
  42.8 6.5 %collective-permute-done.9.refs_1_ = s16[128,512]{1,0:T(8,128)(2,1)S(1)} collective-permute-done((s16[128,512]{1,0:T(8,128)(2,1)S(1)}, s16[128,512]{1,0:T(8,128)(2,1)S(1)}, u32[]{:S(2)}, u32[]{:S(2)}) %collective-permute-start.9) | collective-permute-done | bytes 131104 | tf_op jit(solution)/shard_map/ppermute | solution.py:22
  49.3 3.3 %collective-permute-done.10.refs_2_ = s16[128,512]{1,0:T(8,128)(2,1)S(1)} collective-permute-done((s16[128,512]{1,0:T(8,128)(2,1)S(1)}, s16[128,512]{1,0:T(8,128)(2,1)S(1)}, u32[]{:S(2)}, u32[]{:S(2)}) %collective-permute-start.10) | collective-permute-done | bytes 131104 | tf_op jit(solution)/shard_map/ppermute | solution.py:22
  52.6 0.9 %add_up.1 = f32[16,2,4,512]{3,2,1,0:T(4,128)} custom-call(f32[128,512]{1,0:T(8,128)S(1)} %get-tuple-element.43.own_ref, s16[128,512]{1,0:T(8,128)(2,1)S(1)} %collective-permute-done.8.refs_0_, s16[128,512]{1,0:T(8,128)(2,1)S(1)} %collective-permute-done.9.refs_1_, s16[128,512]{1,0:T(8,128)(2,1)S(1)} %collective-permute-done.10.refs_2_), custom_call_target="tpu_custom_call" | custom-call | tf_op jit(solution)/shard_map/add_up/pallas_call | solution.py:319
Async XLA Ops:
  1.0 7.3 %collective-permute-start.1 = (bf16[64,2048]{1,0:T(8,128)(2,1)S(1)}, bf16[64,2048]{1,0:T(8,128)(2,1)S(1)}, u32[]{:S(2)}, u32[]{:S(2)}) collective-permute-start(bf16[64,2048]{1,0:T(8,128)(2,1)S(1)} %reshape.3.refs_0_), channel_id=1, source_target_pairs={{0,8},{4,12},{8,0},{12,4},{16,24},{20,28},{24,16},{28,20},{1,9},{5... | collective-permute-start | bytes 786440 | tf_op jit(solution)/shard_map/ppermute | solution.py:22
  1.3 6.9 %collective-permute-start.2 = (bf16[64,2048]{1,0:T(8,128)(2,1)S(1)}, bf16[64,2048]{1,0:T(8,128)(2,1)S(1)}, u32[]{:S(2)}, u32[]{:S(2)}) collective-permute-start(bf16[64,2048]{1,0:T(8,128)(2,1)S(1)} %reshape.3.refs_0_), channel_id=1, source_target_pairs={{0,16},{4,20},{8,24},{12,28},{16,0},{20,4},{24,8},{28,12},{1,17},{... | collective-permute-start | bytes 786440 | tf_op jit(solution)/shard_map/ppermute | solution.py:22
  8.3 7.0 %collective-permute-start.5 = (bf16[64,2048]{1,0:T(8,128)(2,1)S(1)}, bf16[64,2048]{1,0:T(8,128)(2,1)S(1)}, u32[]{:S(2)}, u32[]{:S(2)}) collective-permute-start(bf16[64,2048]{1,0:T(8,128)(2,1)S(1)} %reshape.3.refs_0_), channel_id=1, source_target_pairs={{0,24},{4,28},{8,16},{12,20},{16,8},{20,12},{24,0},{28,4},{1,25},{... | collective-permute-start | bytes 786440 | tf_op jit(solution)/shard_map/ppermute | solution.py:22
  10.4 12.8 %collective-permute-start = (bf16[64,2048]{1,0:T(8,128)(2,1)S(1)}, bf16[64,2048]{1,0:T(8,128)(2,1)S(1)}, u32[]{:S(2)}, u32[]{:S(2)}) collective-permute-start(bf16[64,2048]{1,0:T(8,128)(2,1)S(1)} %reshape.3.refs_0_), channel_id=1, source_target_pairs={{0,4},{4,0},{8,12},{12,8},{16,20},{20,16},{24,28},{28,24},{1,5},{5... | collective-permute-start | bytes 786440 | tf_op jit(solution)/shard_map/ppermute | solution.py:22
  12.5 14.8 %collective-permute-start.3 = (bf16[64,2048]{1,0:T(8,128)(2,1)S(1)}, bf16[64,2048]{1,0:T(8,128)(2,1)S(1)}, u32[]{:S(2)}, u32[]{:S(2)}) collective-permute-start(bf16[64,2048]{1,0:T(8,128)(2,1)S(1)} %collective-permute-done.1.refs_2_), channel_id=1, source_target_pairs={{0,4},{4,0},{8,12},{12,8},{16,20},{20,16},{24,28},{28,24},{1,5},{5... | collective-permute-start | bytes 786440 | tf_op jit(solution)/shard_map/ppermute | solution.py:22
  12.5 14.8 %collective-permute-start.4 = (bf16[64,2048]{1,0:T(8,128)(2,1)S(1)}, bf16[64,2048]{1,0:T(8,128)(2,1)S(1)}, u32[]{:S(2)}, u32[]{:S(2)}) collective-permute-start(bf16[64,2048]{1,0:T(8,128)(2,1)S(1)} %collective-permute-done.2.refs_3_), channel_id=1, source_target_pairs={{0,4},{4,0},{8,12},{12,8},{16,20},{20,16},{24,28},{28,24},{1,5},{5... | collective-permute-start | bytes 786440 | tf_op jit(solution)/shard_map/ppermute | solution.py:22
  15.3 12.1 %collective-permute-start.6 = (bf16[64,2048]{1,0:T(8,128)(2,1)S(1)}, bf16[64,2048]{1,0:T(8,128)(2,1)S(1)}, u32[]{:S(2)}, u32[]{:S(2)}) collective-permute-start(bf16[64,2048]{1,0:T(8,128)(2,1)S(1)} %collective-permute-done.5.refs_2_), channel_id=1, source_target_pairs={{0,4},{4,0},{8,12},{12,8},{16,20},{20,16},{24,28},{28,24},{1,5},{5... | collective-permute-start | bytes 786440 | tf_op jit(solution)/shard_map/ppermute | solution.py:22
  17.9 0.7 %copy-start = (s32[512]{0:T(512)S(1)}, s32[512]{0:T(512)}, u32[]{:S(2)}) copy-start(s32[512]{0:T(512)} %param.7) | copy-start | bytes 6148
  18.6 0.7 %copy-start.1 = (s32[64]{0:T(128)S(1)}, s32[64]{0:T(128)}, u32[]{:S(2)}) copy-start(s32[64]{0:T(128)} %frequency_ref.1) | copy-start | bytes 772
  28.0 8.6 %collective-permute-start.7 = (s16[512,256]{1,0:T(8,128)(2,1)S(1)}, s16[512,256]{1,0:T(8,128)(2,1)S(1)}, u32[]{:S(2)}, u32[]{:S(2)}) collective-permute-start(s16[512,256]{1,0:T(8,128)(2,1)S(1)} %heads.1), channel_id=1, source_target_pairs={{4,0},{8,4},{12,8},{16,12},{20,16},{24,20},{28,24},{5,1},{9,5},{13... | collective-permute-start | bytes 786440 | tf_op jit(solution)/shard_map/ppermute | solution.py:367
  37.8 5.0 %collective-permute-start.8 = (s16[128,512]{1,0:T(8,128)(2,1)S(1)}, s16[128,512]{1,0:T(8,128)(2,1)S(1)}, u32[]{:S(2)}, u32[]{:S(2)}) collective-permute-start(s16[128,512]{1,0:T(8,128)(2,1)S(1)} %get-tuple-element.44), channel_id=1, source_target_pairs={{0,1},{1,0},{2,3},{3,2},{4,5},{5,4},{6,7},{7,6},{8,9},{9,8},{10,11... | collective-permute-start | bytes 393224 | tf_op jit(solution)/shard_map/ppermute | solution.py:22
  38.1 11.2 %collective-permute-start.9 = (s16[128,512]{1,0:T(8,128)(2,1)S(1)}, s16[128,512]{1,0:T(8,128)(2,1)S(1)}, u32[]{:S(2)}, u32[]{:S(2)}) collective-permute-start(s16[128,512]{1,0:T(8,128)(2,1)S(1)} %get-tuple-element.45), channel_id=1, source_target_pairs={{0,2},{1,3},{2,0},{3,1},{4,6},{5,7},{6,4},{7,5},{8,10},{9,11},{10,... | collective-permute-start | bytes 393224 | tf_op jit(solution)/shard_map/ppermute | solution.py:22
  40.3 12.3 %collective-permute-start.10 = (s16[128,512]{1,0:T(8,128)(2,1)S(1)}, s16[128,512]{1,0:T(8,128)(2,1)S(1)}, u32[]{:S(2)}, u32[]{:S(2)}) collective-permute-start(s16[128,512]{1,0:T(8,128)(2,1)S(1)} %get-tuple-element.46), channel_id=1, source_target_pairs={{0,3},{1,2},{2,1},{3,0},{4,7},{5,6},{6,5},{7,4},{8,11},{9,10},{10,... | collective-permute-start | bytes 393224 | tf_op jit(solution)/shard_map/ppermute | solution.py:22
